TPU v7x, 512 devices: a whole 4x8x8 slice. The times are simulated.
512 devices in a mesh: group: 32 (over y, x), section: 16 (over z, core).
Axes of the slice: x: 4, y: 8, z: 8, core: 2. Of those that a mesh axis runs over, the one named last changes fastest.
Arguments:
- columns: float32 [32, 32, 16, 8192], P('group', None, None, 'section'), may hold values from -6 to 6
- vectors: bfloat16 [32, 8, 128, 8192], P('group', None, None, 'section'), may hold values from -0.0625 to 0.0625
- factors: float32 [32, 8, 128, 128], P('group'), as said below
- order: int32 [32], P('group'), may hold values from 4096 to 8192
- blocks: int32 [32], P('group'), may hold values from 1 to 8
- live: int32 [32, 32], P('group'), may hold values from 0 to 16
Outputs:
- result: float32 [32, 32, 16, 8192], P('group', None, None, 'section')
Inputs may be any that keep to these rules, and one draw needn't show every extreme that they name: `factors`: upper triangular, diagonal entries between one half and two, off-diagonal entries small.
All inputs are finite; a program needn't handle non-finite values.
Results may differ from a plain program's by a relative error of at most 0.0003.
Values sent between devices are 32-bit elements; how exact they have to be, the bound alone decides.
A program may use at most 64 MiB of HBM per device.

v0:
```python
import jax
import jax.numpy as jnp
from jax import lax
from jax.sharding import Mesh
from jax.sharding import PartitionSpec as P

SECTION = ("section_0", "section_1")


def total_of_pieces(shard, axis):
    return lax.all_gather(shard, axis).sum(0)


def filled_up(lines, size):
    spare = -lines.shape[0] % size
    if not spare:
        return lines
    return jnp.concatenate([lines, jnp.zeros((spare, *lines.shape[1:]), lines.dtype)])


def from_everyone(shard, axis):
    size = lax.axis_size(axis)
    return lax.all_to_all(
        jnp.broadcast_to(shard[None], (size, *shard.shape)), axis, 0, 0, tiled=True
    )


def laid_out(parts, dim):
    parts = jnp.moveaxis(parts, 0, dim)
    lengths = parts.shape
    return parts.reshape(*lengths[:dim], lengths[dim] * lengths[dim + 1], *lengths[dim + 2 :])


def whole_of(shard, axes, dim):
    far, near = axes
    leading = from_everyone(shard, far)
    parts = jnp.swapaxes(from_everyone(leading, near), 0, 1)
    return laid_out(parts.reshape(-1, *shard.shape), dim)


def cut_along(shard, dim, size):
    lengths = shard.shape
    parts = shard.reshape(*lengths[:dim], size, lengths[dim] // size, *lengths[dim + 1 :])
    return jnp.moveaxis(parts, dim, 0)


def summed_on_arrival(shard, axis, dim):
    parts = cut_along(shard, dim, lax.axis_size(axis))
    arrived = lax.all_to_all(parts, axis, split_axis=0, concat_axis=0, tiled=True)
    return arrived.sum(axis=0)


def sum_in_two_steps(shard, axes, dim):
    far, near = axes
    own = summed_on_arrival(cut_along(shard, dim, lax.axis_size(far)), near, dim + 1)
    return jnp.sum(lax.all_to_all(own, far, 0, 0, tiled=True), axis=0)


def nested_sum(shard, axes):
    lines = shard.reshape(-1, shard.shape[-1])
    padded = filled_up(lines, lax.axis_size(axes[0]) * lax.axis_size(axes[1]))
    whole = whole_of(sum_in_two_steps(padded, axes, 0), axes, 0)
    return lax.slice_in_dim(whole, 0, len(lines)).reshape(shard.shape)


def shards(columns, vectors, factors, order, blocks, live):
    count = vectors.shape[1]
    width = vectors.shape[2]
    rows = vectors.shape[3]
    slots = columns.shape[2]
    first_row = lax.axis_index(SECTION) * rows
    inside = (first_row + jnp.arange(rows) < order[0]).astype(jnp.float32)
    basis_all = vectors[0].astype(jnp.float32) * inside[None, None, :]
    active = (jnp.arange(count) < blocks[0]).astype(jnp.float32)
    factor_all = factors[0] * active[:, None, None]
    high = lax.Precision.HIGHEST
    local_correlation = jnp.einsum("jar,jbr->jab", basis_all[0::2], basis_all[1::2], precision=high)
    correlation_all = total_of_pieces(local_correlation, SECTION)
    merged = []
    zeros = jnp.zeros((width, width), jnp.float32)
    for pair in range(count // 2):
        upper_t = factor_all[2 * pair]
        lower_t = factor_all[2 * pair + 1]
        corner = -jnp.dot(
            jnp.dot(upper_t, correlation_all[pair], precision=high), lower_t, precision=high
        )
        top = jnp.concatenate([upper_t, corner], axis=1)
        bottom = jnp.concatenate([zeros, lower_t], axis=1)
        joined = jnp.concatenate([basis_all[2 * pair], basis_all[2 * pair + 1]], axis=0)
        merged.append((joined, jnp.concatenate([top, bottom], axis=0)))
    held = lax.all_to_all(columns[0], "group", split_axis=0, concat_axis=0, tiled=True)
    shape = held.shape
    panel = held.reshape(shape[0] * shape[1], shape[2])
    transform_panel = panel
    for pair in reversed(range(count // 2)):
        joined, factor = merged[pair]
        inner = nested_sum(
            jnp.dot(transform_panel, joined.T, precision=high), ("section_0", "section_1")
        )
        scaled = jnp.dot(inner, factor.T, precision=high)
        transform_panel = transform_panel - jnp.dot(scaled, joined, precision=high)
    moved = transform_panel.reshape(shape)
    returned = lax.all_to_all(moved, "group", split_axis=0, concat_axis=0, tiled=True)
    keep = jnp.arange(slots)[None, :] < live[0][:, None]
    return jnp.where(keep[:, :, None], returned, jnp.float32(0.0))[None]


def solution(mesh):
    finer = Mesh(
        mesh.devices.reshape(mesh.shape["group"], 8, 2), ("group", "section_0", "section_1")
    )
    placed = (
        P("group", None, None, SECTION),
        P("group", None, None, SECTION),
        P("group", None, None, None),
        P("group"),
        P("group"),
        P("group", None),
    )
    return jax.shard_map(
        shards,
        mesh=finer,
        in_specs=placed,
        out_specs=P("group", None, None, SECTION),
        check_vma=False,
    )
```

profile of v0, /device:TPU:1, one launch (start us, length us, event | category | flops | bytes accessed | tf_op | source)
XLA Modules:
  0.0 274.0 jit_solution(14340715749536877685)
XLA Ops:
  7.2 1.5 convert_multiply_fusion
  8.7 1.8 fusion
  10.5 10.5 %all-to-all-start = ((f32[32,16,512]{2,1,0:T(8,128)}), f32[32,16,512]{2,1,0:T(8,128)S(1)}, u32[]{:S(2)}, u32[]{:S(2)}) async-start(f32[32,16,512]{2,1,0:T(8,128)} %bitcast.127), calls=%async_computation | async-start | bytes 2097152 | tf_op jit(solution)/shard_map/all_to_all | solution.py:91
  22.4 24.9 %all-to-all-done = f32[32,16,512]{2,1,0:T(8,128)S(1)} async-done(((f32[32,16,512]{2,1,0:T(8,128)}), f32[32,16,512]{2,1,0:T(8,128)S(1)}, u32[]{:S(2)}, u32[]{:S(2)}) %all-to-all-start) | async-done | bytes 1048608 | tf_op jit(solution)/shard_map/all_to_all | solution.py:91
  47.3 2.1 convolution_bitcast_fusion
  49.6 6.6 %all_to_all.90 = f32[2,8,32,256]{3,2,1,0:T(8,128)S(1)} all-to-all(f32[2,8,32,256]{3,2,1,0:T(8,128)S(1)} %copy.19), channel_id=1, replica_groups=mesh['group'=32,'section_0'=8,'section_1'=2] {'section_1'}, dimensions={0} | all-to-all | bytes 1048576 | tf_op jit(solution)/shard_map/all_to_all | solution.py:49
  57.0 10.0 %all-to-all-start.2 = ((f32[8,32,256]{2,1,0:T(8,128)}), f32[8,32,256]{2,1,0:T(8,128)S(1)}, u32[]{:S(2)}, u32[]{:S(2)}) async-start(f32[8,32,256]{2,1,0:T(8,128)} %reduce_sum.81), calls=%async_computation.2 | async-start | bytes 524288 | tf_op jit(solution)/shard_map/all_to_all | solution.py:56
  67.8 10.2 %all-to-all-done.2 = f32[8,32,256]{2,1,0:T(8,128)S(1)} async-done(((f32[8,32,256]{2,1,0:T(8,128)}), f32[8,32,256]{2,1,0:T(8,128)S(1)}, u32[]{:S(2)}, u32[]{:S(2)}) %all-to-all-start.2) | async-done | bytes 262176 | tf_op jit(solution)/shard_map/all_to_all | solution.py:56
  78.8 3.4 %all-to-all-start.3 = ((f32[8,32,256]{2,1,0:T(8,128)}), f32[8,32,256]{2,1,0:T(8,128)S(1)}, u32[]{:S(2)}, u32[]{:S(2)}) async-start(f32[8,32,256]{2,1,0:T(8,128)} %broadcast_in_dim.27), calls=%async_computation.3 | async-start | bytes 524288 | tf_op jit(solution)/shard_map/all_to_all | solution.py:23
  83.2 8.8 %all-to-all-done.3 = f32[8,32,256]{2,1,0:T(8,128)S(1)} async-done(((f32[8,32,256]{2,1,0:T(8,128)}), f32[8,32,256]{2,1,0:T(8,128)S(1)}, u32[]{:S(2)}, u32[]{:S(2)}) %all-to-all-start.3) | async-done | bytes 262176 | tf_op jit(solution)/shard_map/all_to_all | solution.py:23
  92.0 6.8 %all_to_all.91 = f32[2,8,32,256]{3,2,1,0:T(8,128)S(1)} all-to-all(f32[2,8,32,256]{3,2,1,0:T(8,128)S(1)} %broadcast_in_dim.28), channel_id=1, replica_groups=mesh['group'=32,'section_0'=8,'section_1'=2] {'section_1'}, dimensions={0} | all-to-all | bytes 1048576 | tf_op jit(solution)/shard_map/all_to_all | solution.py:23
  98.9 2.5 reduce_sum.83
  102.7 2.0 convolution_subtract_fusion.3
  105.8 4.2 %all_to_all.92 = f32[2,8,32,256]{3,2,1,0:T(8,128)S(1)} all-to-all(f32[2,8,32,256]{3,2,1,0:T(8,128)S(1)} %bitcast.121), channel_id=1, replica_groups=mesh['group'=32,'section_0'=8,'section_1'=2] {'section_1'}, dimensions={0} | all-to-all | bytes 1048576 | tf_op jit(solution)/shard_map/all_to_all | solution.py:49
  110.0 14.7 %all_to_all.93 = f32[8,32,256]{2,1,0:T(8,128)S(1)} all-to-all(f32[8,32,256]{2,1,0:T(8,128)S(1)} %reduce_sum.84), channel_id=1, replica_groups=mesh['group'=32,'section_0'=8,'section_1'=2] {'section_0'}, dimensions={0} | all-to-all | bytes 524288 | tf_op jit(solution)/shard_map/all_to_all | solution.py:56
  125.5 3.4 %all-to-all-start.7 = ((f32[8,32,256]{2,1,0:T(8,128)}), f32[8,32,256]{2,1,0:T(8,128)S(1)}, u32[]{:S(2)}, u32[]{:S(2)}) async-start(f32[8,32,256]{2,1,0:T(8,128)} %broadcast_in_dim.29), calls=%async_computation.7 | async-start | bytes 524288 | tf_op jit(solution)/shard_map/all_to_all | solution.py:23
  130.9 9.7 %all-to-all-done.7 = f32[8,32,256]{2,1,0:T(8,128)S(1)} async-done(((f32[8,32,256]{2,1,0:T(8,128)}), f32[8,32,256]{2,1,0:T(8,128)S(1)}, u32[]{:S(2)}, u32[]{:S(2)}) %all-to-all-start.7) | async-done | bytes 262176 | tf_op jit(solution)/shard_map/all_to_all | solution.py:23
  140.7 4.8 %all_to_all.94 = f32[2,8,32,256]{3,2,1,0:T(8,128)S(1)} all-to-all(f32[2,8,32,256]{3,2,1,0:T(8,128)S(1)} %broadcast_in_dim.30), channel_id=1, replica_groups=mesh['group'=32,'section_0'=8,'section_1'=2] {'section_1'}, dimensions={0} | all-to-all | bytes 1048576 | tf_op jit(solution)/shard_map/all_to_all | solution.py:23
  145.6 1.5 fusion.10
  149.2 4.3 %all_to_all.95 = f32[2,8,32,256]{3,2,1,0:T(8,128)S(1)} all-to-all(f32[2,8,32,256]{3,2,1,0:T(8,128)S(1)} %bitcast.122), channel_id=1, replica_groups=mesh['group'=32,'section_0'=8,'section_1'=2] {'section_1'}, dimensions={0} | all-to-all | bytes 1048576 | tf_op jit(solution)/shard_map/all_to_all | solution.py:49
  153.6 14.7 %all_to_all.96 = f32[8,32,256]{2,1,0:T(8,128)S(1)} all-to-all(f32[8,32,256]{2,1,0:T(8,128)S(1)} %reduce_sum.86), channel_id=1, replica_groups=mesh['group'=32,'section_0'=8,'section_1'=2] {'section_0'}, dimensions={0} | all-to-all | bytes 524288 | tf_op jit(solution)/shard_map/all_to_all | solution.py:56
  169.0 3.6 %all-to-all-start.11 = ((f32[8,32,256]{2,1,0:T(8,128)}), f32[8,32,256]{2,1,0:T(8,128)S(1)}, u32[]{:S(2)}, u32[]{:S(2)}) async-start(f32[8,32,256]{2,1,0:T(8,128)} %broadcast_in_dim.31), calls=%async_computation.11 | async-start | bytes 524288 | tf_op jit(solution)/shard_map/all_to_all | solution.py:23
  174.0 10.1 %all-to-all-done.11 = f32[8,32,256]{2,1,0:T(8,128)S(1)} async-done(((f32[8,32,256]{2,1,0:T(8,128)}), f32[8,32,256]{2,1,0:T(8,128)S(1)}, u32[]{:S(2)}, u32[]{:S(2)}) %all-to-all-start.11) | async-done | bytes 262176 | tf_op jit(solution)/shard_map/all_to_all | solution.py:23
  184.2 4.9 %all_to_all.97 = f32[2,8,32,256]{3,2,1,0:T(8,128)S(1)} all-to-all(f32[2,8,32,256]{3,2,1,0:T(8,128)S(1)} %broadcast_in_dim.32), channel_id=1, replica_groups=mesh['group'=32,'section_0'=8,'section_1'=2] {'section_1'}, dimensions={0} | all-to-all | bytes 1048576 | tf_op jit(solution)/shard_map/all_to_all | solution.py:23
  192.0 4.2 %all_to_all.98 = f32[2,8,32,256]{3,2,1,0:T(8,128)S(1)} all-to-all(f32[2,8,32,256]{3,2,1,0:T(8,128)S(1)} %bitcast.123), channel_id=1, replica_groups=mesh['group'=32,'section_0'=8,'section_1'=2] {'section_1'}, dimensions={0} | all-to-all | bytes 1048576 | tf_op jit(solution)/shard_map/all_to_all | solution.py:49
  196.2 14.7 %all_to_all.99 = f32[8,32,256]{2,1,0:T(8,128)S(1)} all-to-all(f32[8,32,256]{2,1,0:T(8,128)S(1)} %reduce_sum.88), channel_id=1, replica_groups=mesh['group'=32,'section_0'=8,'section_1'=2] {'section_0'}, dimensions={0} | all-to-all | bytes 524288 | tf_op jit(solution)/shard_map/all_to_all | solution.py:56
  211.6 3.4 %all-to-all-start.15 = ((f32[8,32,256]{2,1,0:T(8,128)}), f32[8,32,256]{2,1,0:T(8,128)S(1)}, u32[]{:S(2)}, u32[]{:S(2)}) async-start(f32[8,32,256]{2,1,0:T(8,128)} %broadcast_in_dim.33), calls=%async_computation.15 | async-start | bytes 524288 | tf_op jit(solution)/shard_map/all_to_all | solution.py:23
  217.1 9.7 %all-to-all-done.15 = f32[8,32,256]{2,1,0:T(8,128)S(1)} async-done(((f32[8,32,256]{2,1,0:T(8,128)}), f32[8,32,256]{2,1,0:T(8,128)S(1)}, u32[]{:S(2)}, u32[]{:S(2)}) %all-to-all-start.15) | async-done | bytes 262176 | tf_op jit(solution)/shard_map/all_to_all | solution.py:23
  226.8 4.8 %all_to_all.100 = f32[2,8,32,256]{3,2,1,0:T(8,128)S(1)} all-to-all(f32[2,8,32,256]{3,2,1,0:T(8,128)S(1)} %broadcast_in_dim.34), channel_id=1, replica_groups=mesh['group'=32,'section_0'=8,'section_1'=2] {'section_1'}, dimensions={0} | all-to-all | bytes 1048576 | tf_op jit(solution)/shard_map/all_to_all | solution.py:23
  232.3 2.0 convolution_subtract_fusion
  234.3 5.3 %all-to-all-start.17 = ((f32[32,16,512]{2,1,0:T(8,128)}), f32[32,16,512]{2,1,0:T(8,128)S(1)}, u32[]{:S(2)}, u32[]{:S(2)}) async-start(f32[32,16,512]{2,1,0:T(8,128)} %bitcast.45), calls=%async_computation.17 | async-start | bytes 2097152 | tf_op jit(solution)/shard_map/all_to_all | solution.py:103
  239.7 26.3 %all-to-all-done.17 = f32[32,16,512]{2,1,0:T(8,128)S(1)} async-done(((f32[32,16,512]{2,1,0:T(8,128)}), f32[32,16,512]{2,1,0:T(8,128)S(1)}, u32[]{:S(2)}, u32[]{:S(2)}) %all-to-all-start.17) | async-done | bytes 1048608 | tf_op jit(solution)/shard_map/all_to_all | solution.py:103
  (90 shorter events, 21.1 us)
Async XLA Ops:
  6.5 92.4 %all-gather.3.cloned.1.call-start = ((), (), s32[]{:S(2)}) async-start(), calls=%async_computation.18 | async-start | bytes 4456448 | tf_op jit(solution)/shard_map/all_gather | solution.py:11
  10.5 36.7 %all-to-all-start = ((f32[32,16,512]{2,1,0:T(8,128)}), f32[32,16,512]{2,1,0:T(8,128)S(1)}, u32[]{:S(2)}, u32[]{:S(2)}) async-start(f32[32,16,512]{2,1,0:T(8,128)} %bitcast.127), calls=%async_computation | async-start | bytes 2097152 | tf_op jit(solution)/shard_map/all_to_all | solution.py:91
  49.3 17.6 %copy-start.11 = (f32[1,8,128,128]{3,2,1,0:T(8,128)S(1)}, f32[1,8,128,128]{3,2,1,0:T(8,128)}, u32[]{:S(2)}) copy-start(f32[1,8,128,128]{3,2,1,0:T(8,128)} %param.8) | copy-start | bytes 1572868
  57.0 21.1 %all-to-all-start.2 = ((f32[8,32,256]{2,1,0:T(8,128)}), f32[8,32,256]{2,1,0:T(8,128)S(1)}, u32[]{:S(2)}, u32[]{:S(2)}) async-start(f32[8,32,256]{2,1,0:T(8,128)} %reduce_sum.81), calls=%async_computation.2 | async-start | bytes 524288 | tf_op jit(solution)/shard_map/all_to_all | solution.py:56
  78.8 13.1 %all-to-all-start.3 = ((f32[8,32,256]{2,1,0:T(8,128)}), f32[8,32,256]{2,1,0:T(8,128)S(1)}, u32[]{:S(2)}, u32[]{:S(2)}) async-start(f32[8,32,256]{2,1,0:T(8,128)} %broadcast_in_dim.27), calls=%async_computation.3 | async-start | bytes 524288 | tf_op jit(solution)/shard_map/all_to_all | solution.py:23
  82.4 47.7 %copy-start = (f32[8,128,128]{1,2,0:T(8,128)}, f32[8,128,128]{1,2,0:T(8,128)S(1)}, u32[]{:S(2)}) copy-start(f32[8,128,128]{1,2,0:T(8,128)S(1)} %bitcast_multiply_fusion) | copy-start | bytes 1572868
  98.9 3.2 %copy-start.14 = (f32[128,128]{0,1:T(8,128)S(1)}, f32[128,128]{0,1:T(8,128)}, u32[]{:S(2)}) copy-start(f32[128,128]{0,1:T(8,128)} %get-tuple-element.19) | copy-start | bytes 196612
  98.9 3.2 %copy-start.15 = (f32[128,128]{0,1:T(8,128)S(1)}, f32[128,128]{0,1:T(8,128)}, u32[]{:S(2)}) copy-start(f32[128,128]{0,1:T(8,128)} %get-tuple-element.20) | copy-start | bytes 196612
  101.4 0.7 copy-start.10
  102.1 2.7 copy-start.6
  102.1 2.7 copy-start.8
  125.5 15.1 %all-to-all-start.7 = ((f32[8,32,256]{2,1,0:T(8,128)}), f32[8,32,256]{2,1,0:T(8,128)S(1)}, u32[]{:S(2)}, u32[]{:S(2)}) async-start(f32[8,32,256]{2,1,0:T(8,128)} %broadcast_in_dim.29), calls=%async_computation.7 | async-start | bytes 524288 | tf_op jit(solution)/shard_map/all_to_all | solution.py:23
  130.9 16.1 %copy-start.7 = (f32[128,512]{1,0:T(8,128)S(1)}, f32[128,512]{1,0:T(8,128)}, u32[]{:S(2)}) copy-start(f32[128,512]{1,0:T(8,128)} %get-tuple-element.8) | copy-start | bytes 786436
  130.9 16.2 %copy-start.9 = (f32[128,512]{1,0:T(8,128)S(1)}, f32[128,512]{1,0:T(8,128)}, u32[]{:S(2)}) copy-start(f32[128,512]{1,0:T(8,128)} %get-tuple-element.9) | copy-start | bytes 786436
  140.6 4.9 %copy-start.17 = (f32[128,128]{0,1:T(8,128)S(1)}, f32[128,128]{0,1:T(8,128)}, u32[]{:S(2)}) copy-start(f32[128,128]{0,1:T(8,128)} %convolution_negate_fusion.2) | copy-start | bytes 196612
  145.5 2.6 copy-start.3
  145.6 2.6 copy-start.4
  149.2 23.5 %copy-start.1 = (f32[8,128,128]{1,2,0:T(8,128)S(1)}, f32[8,128,128]{1,2,0:T(8,128)}, u32[]{:S(2)}) copy-start(f32[8,128,128]{1,2,0:T(8,128)} %copy-done) | copy-start | bytes 1572868
  168.3 20.9 %copy-start.12 = (f32[128,128]{0,1:T(8,128)S(1)}, f32[128,128]{0,1:T(8,128)}, u32[]{:S(2)}) copy-start(f32[128,128]{0,1:T(8,128)} %get-tuple-element.15) | copy-start | bytes 196612
  168.3 20.9 %copy-start.13 = (f32[128,128]{0,1:T(8,128)S(1)}, f32[128,128]{0,1:T(8,128)}, u32[]{:S(2)}) copy-start(f32[128,128]{0,1:T(8,128)} %get-tuple-element.16) | copy-start | bytes 196612
  169.0 15.1 %all-to-all-start.11 = ((f32[8,32,256]{2,1,0:T(8,128)}), f32[8,32,256]{2,1,0:T(8,128)S(1)}, u32[]{:S(2)}, u32[]{:S(2)}) async-start(f32[8,32,256]{2,1,0:T(8,128)} %broadcast_in_dim.31), calls=%async_computation.11 | async-start | bytes 524288 | tf_op jit(solution)/shard_map/all_to_all | solution.py:23
  184.2 5.7 %copy-start.5 = (f32[128,512]{1,0:T(8,128)S(1)}, f32[128,512]{1,0:T(8,128)}, u32[]{:S(2)}) copy-start(f32[128,512]{1,0:T(8,128)} %get-tuple-element.7) | copy-start | bytes 786436
  189.2 1.6 copy-start.2
  211.6 15.1 %all-to-all-start.15 = ((f32[8,32,256]{2,1,0:T(8,128)}), f32[8,32,256]{2,1,0:T(8,128)S(1)}, u32[]{:S(2)}, u32[]{:S(2)}) async-start(f32[8,32,256]{2,1,0:T(8,128)} %broadcast_in_dim.33), calls=%async_computation.15 | async-start | bytes 524288 | tf_op jit(solution)/shard_map/all_to_all | solution.py:23
  217.1 14.6 %copy-start.16 = (f32[128,128]{0,1:T(8,128)S(1)}, f32[128,128]{0,1:T(8,128)}, u32[]{:S(2)}) copy-start(f32[128,128]{0,1:T(8,128)} %convolution_negate_fusion) | copy-start | bytes 196612
  232.3 7.3 %copy-start.18 = (s32[1,32]{1,0:T(1,128)S(1)}, s32[1,32]{1,0:T(1,128)}, u32[]{:S(2)}) copy-start(s32[1,32]{1,0:T(1,128)} %param.11) | copy-start | bytes 388
  234.3 31.7 %all-to-all-start.17 = ((f32[32,16,512]{2,1,0:T(8,128)}), f32[32,16,512]{2,1,0:T(8,128)S(1)}, u32[]{:S(2)}, u32[]{:S(2)}) async-start(f32[32,16,512]{2,1,0:T(8,128)} %bitcast.45), calls=%async_computation.17 | async-start | bytes 2097152 | tf_op jit(solution)/shard_map/all_to_all | solution.py:103
Sparse Core Ops, SparseCore 0:
  10.7 51.0 all-gather.2
where the time goes:
time: 277 us; the launch traced here: 274 us
  waiting for transfers between devices  99.8 us (36%)
  blocking collectives  84.8 us (31%)
  starting transfers between devices  39.6 us (14%)
  matrix products  22.2 us (8%)
  between operations  15.3 us (6%)
  other arithmetic  6.18 us (2%)
  local copies, waits for them, and re-layouts  6.08 us (2%)
    all_to_all x3, blocking collectives, sum_in_two_steps(): return jnp.sum(lax.all_to_all(own, far, 0, 0, tiled=True), axis=0)  44.2 us
    all_to_all x4, waiting for transfers between devices, from_everyone(): lax.all_to_all(jnp.broadcast_to(shard[None], (size, *shard.shape)), axis,...  38.3 us
    all_to_all x1, waiting for transfers between devices, shards(): lax.all_to_all(moved, 'group', split_axis=0, concat_axis=0, tiled=True)  26.3 us
    all_to_all x1, waiting for transfers between devices, shards(): lax.all_to_all(columns[0], 'group', split_axis=0, concat_axis=0, tiled=True)  24.9 us
    all_to_all x4, blocking collectives, from_everyone(): lax.all_to_all(jnp.broadcast_to(shard[None], (size, *shard.shape)), axis,...  21.4 us
    all_to_all x4, blocking collectives, summed_on_arrival(): lax.all_to_all(parts, axis, split_axis=0, concat_axis=0, tiled=True)  19.2 us
    all_to_all x4, starting transfers between devices, from_everyone(): lax.all_to_all(jnp.broadcast_to(shard[None], (size, *shard.shape)), axis,...  13.8 us
    all_to_all x1, starting transfers between devices, shards(): lax.all_to_all(columns[0], 'group', split_axis=0, concat_axis=0, tiled=True)  10.5 us
  transfers between devices with their start and end apart: 8, of which 7 were waited for; matrix products, arithmetic and copies ran while one was open for 4% of the time, Pallas kernels for 0%

commit v1 on v0

v1 whole, which is shorter than its diff:
```python
import functools

import jax
import jax.numpy as jnp
from jax import lax
from jax.experimental import pallas as pl
from jax.experimental.pallas import tpu as pltpu
from jax.sharding import PartitionSpec as P

MESH = pl.DeviceIdType.MESH
F32 = jnp.float32
BF16 = jnp.bfloat16
HIGH = lax.Precision.HIGHEST
STREAMS = 2


def three(x):
    first = x.astype(BF16)
    rest = x - first.astype(F32)
    second = rest.astype(BF16)
    third = (rest - second.astype(F32)).astype(BF16)
    return first, second, third


def times(a, b):
    return jnp.dot(a, b, preferred_element_type=F32)


def exact(a, b):
    return jnp.dot(a, b, precision=HIGH, preferred_element_type=F32)


def against(a, b):
    return lax.dot_general(a, b, (((1,), (1,)), ((), ())), preferred_element_type=F32)


class Place:
    def __init__(self, ring):
        self.ring = ring
        self.long = ring // 2
        self.short = ring - 1 - self.long
        self.group = lax.axis_index("group")
        self.section = lax.axis_index("section")
        self.z = self.section // 2
        self.core = lax.rem(self.section, 2)
        self.way = 1 - 2 * self.core

    def at(self, steps):
        return lax.rem(self.z + self.way * steps + 2 * self.ring, self.ring)

    def neighbour(self, steps):
        return (self.group, self.at(steps) * 2 + self.core)

    def partner(self):
        return (self.group, self.z * 2 + 1 - self.core)


class Sum:
    def __init__(self, place, src, swapped, far, near, full, sent, swap_sem, ring_sem, gather_sem):
        self.p = place
        self.src, self.swapped, self.far, self.near, self.full = src, swapped, far, near, full
        self.sent, self.swap_sem, self.ring_sem, self.gather_sem = sent, swap_sem, ring_sem, gather_sem
        self.rows = far.shape[1]

    def piece(self, ref, z, core):
        start = pl.multiple_of((z * 2 + core) * self.rows, self.rows)
        return ref.at[pl.ds(start, self.rows)]

    def send(self, src, dst, which, recv, device):
        return pltpu.make_async_remote_copy(
            src_ref=src,
            dst_ref=dst,
            send_sem=self.sent.at[which],
            recv_sem=recv,
            device_id=device,
            device_id_type=MESH,
        )

    def arrived(self, dst, recv):
        self.send(dst, dst, 0, recv, self.p.partner()).wait_recv()

    def swap(self):
        p = self.p
        steps = []
        for t in range(p.long):
            steps.append(p.long - t)
            if t < p.short:
                steps.append(t - p.short)
        for k in steps + [0]:
            z = p.at(-k)
            self.send(
                self.piece(self.src, z, 1 - p.core), self.swapped.at[z], 0, self.swap_sem.at[0, z], p.partner()
            ).start()

    def own(self, z):
        self.arrived(self.swapped.at[z], self.swap_sem.at[0, z])
        return self.piece(self.src, z, self.p.core)[...] + self.swapped[z]

    def hop(self, buffers, sem, t, z, device):
        mine = self.own(z)
        if t == 0:
            self.swapped[z] = mine
            source = self.swapped.at[z]
        else:
            self.arrived(buffers.at[t - 1], self.ring_sem.at[sem, t - 1])
            buffers[t - 1] = buffers[t - 1] + mine
            source = buffers.at[t - 1]
        self.send(source, buffers.at[t], 0, self.ring_sem.at[sem, t], device).start()

    def step(self, t):
        p = self.p
        self.hop(self.far, 0, t, p.at(p.long - t), p.neighbour(1))
        if t < p.short:
            self.hop(self.near, 1, t, p.at(t - p.short), p.neighbour(-1))

    def total(self):
        p = self.p
        mine = self.own(p.z)
        self.arrived(self.far.at[p.long - 1], self.ring_sem.at[0, p.long - 1])
        self.arrived(self.near.at[p.short - 1], self.ring_sem.at[1, p.short - 1])
        return mine + self.far[p.long - 1] + self.near[p.short - 1]

    def forward(self, origin, t):
        p = self.p
        piece = self.piece(self.full, origin, p.core)
        if t >= 0 and t < p.long:
            self.send(piece, piece, 1, self.gather_sem.at[0, t], p.neighbour(1)).start()
        if t <= 0 and -t < p.short:
            self.send(piece, piece, 1, self.gather_sem.at[1, -t], p.neighbour(-1)).start()
        self.send(piece, piece, 1, self.swap_sem.at[1, origin], p.partner()).start()

    def spread(self, value):
        p = self.p
        self.piece(self.full, p.z, p.core)[...] = value
        self.forward(p.z, 0)

    def relay(self, t):
        p = self.p
        origin = p.at(-t)
        self.arrived(self.piece(self.full, origin, p.core), self.gather_sem.at[0, t - 1])
        self.forward(origin, t)
        if t <= p.short:
            origin = p.at(t)
            self.arrived(self.piece(self.full, origin, p.core), self.gather_sem.at[1, t - 1])
            self.forward(origin, -t)

    def gathered(self):
        p = self.p
        for z in range(p.ring):
            self.arrived(self.piece(self.full, z, 1 - p.core), self.swap_sem.at[1, z])

    def drain(self):
        pieces = 2 * self.p.ring - 1
        whole = self.full.at[pl.ds(0, pieces * self.rows)]
        for which in range(2):
            self.send(whole, whole, which, self.swap_sem.at[0, 0], self.p.partner()).wait_send()


def kernel(
    groups,
    ring,
    columns,
    vectors,
    factors,
    order,
    blocks,
    out,
    raw,
    facts,
    basis,
    panel,
    moved,
    g_src,
    g_swapped,
    g_far,
    g_near,
    g_full,
    tri,
    tri_parts,
    w_src,
    w_swapped,
    w_far,
    w_near,
    w_full,
    load_sem,
    in_send,
    in_recv,
    out_send,
    out_recv,
    sent,
    swap_sem,
    ring_sem,
    gather_sem,
):
    p = Place(ring)
    me, section = p.group, p.section
    count, width, rows = raw.shape
    slots = panel.shape[1] // groups

    barrier = pltpu.get_barrier_semaphore()

    def greet(d, carry):
        peer = lax.rem(me + d, groups)
        pl.semaphore_signal(barrier, inc=1, device_id=(peer, section), device_id_type=MESH)
        return carry

    lax.fori_loop(1, groups, greet, 0)
    for other in (p.neighbour(1), p.neighbour(-1), p.partner()):
        pl.semaphore_signal(barrier, inc=1, device_id=other, device_id_type=MESH)

    loads = [
        pltpu.make_async_copy(vectors.at[0], raw, load_sem.at[0]),
        pltpu.make_async_copy(factors.at[0], facts, load_sem.at[1]),
    ]
    for s in range(STREAMS):
        loads.append(
            pltpu.make_async_copy(
                columns.at[0, me, pl.ds(s * slots, slots)],
                panel.at[s, pl.ds(pl.multiple_of(me * slots, slots), slots)],
                load_sem.at[2 + s],
            )
        )
    for load in loads:
        load.start()
    tri[...] = jnp.zeros_like(tri)
    loads[0].wait()
    row = section * rows + lax.broadcasted_iota(jnp.int32, (width, rows), 1)
    inside = row < order[0]
    for j in range(count):
        block = jnp.where(inside, raw[j].astype(F32), 0.0)
        basis[pl.ds(j * width, width)] = block.astype(BF16)

    pl.semaphore_wait(barrier, groups + 2)

    def exchange(s, source, target, send_sem, recv_sem):
        def one(k, carry):
            half = (k + 1) // 2
            d = groups // 2 + (2 * lax.rem(k, 2) - 1) * half
            peer = lax.rem(me + d, groups)
            pltpu.make_async_remote_copy(
                src_ref=source(peer),
                dst_ref=target(me),
                send_sem=send_sem,
                recv_sem=recv_sem,
                device_id=(peer, section),
                device_id_type=MESH,
            ).start()
            return carry

        lax.fori_loop(0, groups - 1, one, 0)

    def lines(ref, s):
        return lambda g: ref.at[s, pl.ds(pl.multiple_of(g * slots, slots), slots)]

    def slab(ref, s):
        return lambda g: ref.at[0, g, pl.ds(s * slots, slots)]

    for s in range(STREAMS):
        exchange(s, slab(columns, s), lines(panel, s), in_send.at[s], in_recv.at[s])

    place_of = {}
    for k in range(1, count):
        low = against(basis[pl.ds(k * width, width)], basis[pl.ds(0, k * width)])
        for j in range(k):
            place_of[k, j] = len(place_of)
            g_src[pl.ds(place_of[k, j] * width, width)] = low[:, j * width : (j + 1) * width]

    gram = Sum(p, g_src, g_swapped, g_far, g_near, g_full, sent.at[0], swap_sem.at[0], ring_sem.at[0], gather_sem.at[0])
    parts = [
        Sum(
            p,
            w_src.at[s],
            w_swapped.at[s],
            w_far.at[s],
            w_near.at[s],
            w_full.at[s],
            sent.at[1 + s],
            swap_sem.at[1 + s],
            ring_sem.at[1 + s],
            gather_sem.at[1 + s],
        )
        for s in range(STREAMS)
    ]
    gram.swap()
    loads[1].wait()
    for j in range(count):
        factor = jnp.where(j < blocks[0], facts[j], 0.0)
        tri[pl.ds(j * width, width), pl.ds(j * width, width)] = factor.T
    for t in range(p.long):
        gram.step(t)
    gram.spread(gram.total())
    for t in range(1, p.long + 1):
        gram.relay(t)
    gram.gathered()

    def low_block(first, size):
        lines = []
        for k in range(first + size, first + 2 * size):
            lines.append(
                jnp.concatenate(
                    [g_full[pl.ds(place_of[k, j] * width, width)] for j in range(first, first + size)], axis=1
                )
            )
        return jnp.concatenate(lines, axis=0)

    def merge(first, size):
        top = pl.ds(first * width, size * width)
        low = pl.ds((first + size) * width, size * width)
        tri[low, top] = -exact(tri[low, low], exact(low_block(first, size), tri[top, top]))

    def split():
        for i, part in enumerate(three(tri[...])):
            tri_parts[i] = part

    def peer_lines(s):
        whole = panel.at[s, pl.ds(0, (groups - 1) * slots)]
        return whole

    def bring(s):
        loads[2 + s].wait()
        whole = peer_lines(s)
        pltpu.make_async_remote_copy(
            whole, whole, in_send.at[s], in_recv.at[s], device_id=p.partner(), device_id_type=MESH
        ).wait_recv()
        a, b, c = three(panel[s])
        v = basis[...]
        w_src[s] = against(c, v) + against(b, v) + against(a, v)

    def scaled(total):
        a, b, c = three(total)
        half = tri.shape[0] // 2
        done = []
        for first, last, start in ((0, half, 0), (half, 2 * half, half)):
            t0, t1, t2 = (tri_parts[i, start:, first:last] for i in range(3))
            a_, b_, c_ = a[:, start:], b[:, start:], c[:, start:]
            small = times(c_, t0) + times(b_, t1) + times(a_, t2)
            done.append(small + times(b_, t0) + times(a_, t1) + times(a_, t0))
        return jnp.concatenate(done, axis=1)

    def leave(s):
        a, b, c = three(w_full[s])
        v = basis[...]
        moved[s] = panel[s] - (times(c, v) + times(b, v) + times(a, v))
        exchange(s, lines(moved, s), slab(out, s), out_send.at[s], out_recv.at[s])
        own = pltpu.make_async_copy(lines(moved, s)(me), slab(out, s)(me), load_sem.at[2 + s])
        own.start()
        return own

    bring(0)
    parts[0].swap()
    for first in range(0, count, 2):
        merge(first, 1)
    parts[0].step(0)
    for first in range(0, count, 4):
        merge(first, 2)
    parts[0].step(1)
    merge(0, count // 2)
    for t in range(2, p.long):
        parts[0].step(t)
    split()
    bring(1)
    parts[1].swap()
    parts[0].spread(scaled(parts[0].total()))
    for t in range(p.long):
        parts[1].step(t)
        parts[0].relay(t + 1)
    parts[1].spread(scaled(parts[1].total()))
    parts[0].gathered()
    own0 = leave(0)
    for t in range(p.long):
        parts[1].relay(t + 1)
    parts[1].gathered()
    own1 = leave(1)

    gram.drain()
    for s in range(STREAMS):
        parts[s].drain()
    own0.wait()
    own1.wait()
    for s in range(STREAMS):
        whole = peer_lines(s)
        pltpu.make_async_remote_copy(
            whole, whole, in_send.at[s], in_recv.at[s], device_id=p.partner(), device_id_type=MESH
        ).wait_send()
        there = pltpu.make_async_remote_copy(
            whole, whole, out_send.at[s], out_recv.at[s], device_id=p.partner(), device_id_type=MESH
        )
        there.wait_send()
        there.wait_recv()


def shards(groups, ring, columns, vectors, factors, order, blocks, live):
    _, count, width, rows = vectors.shape
    slots = columns.shape[2]
    each = slots // STREAMS
    lines = groups * each
    merged = count * width
    long, short = ring // 2, ring - 1 - ring // 2
    gram = count * (count - 1) // 2 * width
    g_piece, w_piece = gram // (2 * ring), lines // (2 * ring)
    anywhere = pl.BlockSpec(memory_space=pl.ANY)
    scalars = pl.BlockSpec(memory_space=pltpu.SMEM)
    returned = pl.pallas_call(
        functools.partial(kernel, groups, ring),
        out_shape=jax.ShapeDtypeStruct(columns.shape, F32),
        in_specs=[anywhere, anywhere, anywhere, scalars, scalars],
        out_specs=anywhere,
        scratch_shapes=[
            pltpu.VMEM((count, width, rows), BF16),
            pltpu.VMEM((count, width, width), F32),
            pltpu.VMEM((merged, rows), BF16),
            pltpu.VMEM((STREAMS, lines, rows), F32),
            pltpu.VMEM((STREAMS, lines, rows), F32),
            pltpu.VMEM((gram, width), F32),
            pltpu.VMEM((ring, g_piece, width), F32),
            pltpu.VMEM((long, g_piece, width), F32),
            pltpu.VMEM((short, g_piece, width), F32),
            pltpu.VMEM((gram, width), F32),
            pltpu.VMEM((merged, merged), F32),
            pltpu.VMEM((3, merged, merged), BF16),
            pltpu.VMEM((STREAMS, lines, merged), F32),
            pltpu.VMEM((STREAMS, ring, w_piece, merged), F32),
            pltpu.VMEM((STREAMS, long, w_piece, merged), F32),
            pltpu.VMEM((STREAMS, short, w_piece, merged), F32),
            pltpu.VMEM((STREAMS, lines, merged), F32),
            pltpu.SemaphoreType.DMA((2 + STREAMS,)),
            pltpu.SemaphoreType.DMA((STREAMS,)),
            pltpu.SemaphoreType.DMA((STREAMS,)),
            pltpu.SemaphoreType.DMA((STREAMS,)),
            pltpu.SemaphoreType.DMA((STREAMS,)),
            pltpu.SemaphoreType.DMA((1 + STREAMS, 2)),
            pltpu.SemaphoreType.DMA((1 + STREAMS, 2, ring)),
            pltpu.SemaphoreType.DMA((1 + STREAMS, 2, long)),
            pltpu.SemaphoreType.DMA((1 + STREAMS, 2, long)),
        ],
        compiler_params=pltpu.CompilerParams(
            collective_id=0, has_side_effects=True, vmem_limit_bytes=60 * 1024 * 1024
        ),
        name="back_transform",
    )(columns, vectors, factors, order, blocks)
    keep = jnp.arange(slots)[None, :] < live[0][:, None]
    return jnp.where(keep[None, :, :, None], returned, jnp.float32(0.0))


def solution(mesh):
    groups, ring = mesh.shape["group"], mesh.shape["section"] // 2
    placed = (
        P("group", None, None, "section"),
        P("group", None, None, "section"),
        P("group", None, None, None),
        P("group"),
        P("group"),
        P("group", None),
    )
    return jax.shard_map(
        functools.partial(shards, groups, ring),
        mesh=mesh,
        in_specs=placed,
        out_specs=P("group", None, None, "section"),
        check_vma=False,
    )
```

time: 277 us -> 127 us (0.46)
  Pallas kernels: 0 us -> 122 us
  waiting for transfers between devices: 99.8 us -> 0 us
  blocking collectives: 84.8 us -> 0 us
  starting transfers between devices: 39.6 us -> 0 us
  matrix products: 22.2 us -> 0 us
  between operations: 15.3 us -> 1.31 us
  local copies, waits for them, and re-layouts: 6.08 us -> 0.65 us
  other arithmetic: 6.18 us -> 2.41 us
    pallas_call x0 -> x1, Pallas kernels: none -> 122 us  [shards(): pl.pallas_call(functools.partial(kernel, groups, ring), out_shape=jax.Sha...]
    all_to_all x7 -> x0, waiting for transfers between devices: 99.7 us -> none  [the longest x4 38.3 us: from_everyone(): lax.all_to_all(jnp.broadcast_to(shard[None], (size, *shard.shape)), axis,...]
    all_to_all x11 -> x0, blocking collectives: 84.8 us -> none  [the longest x3 44.2 us: sum_in_two_steps(): return jnp.sum(lax.all_to_all(own, far, 0, 0, tiled=True), axis=0)]
    all_to_all x7 -> x0, starting transfers between devices: 39.6 us -> none  [the longest x4 13.8 us: from_everyone(): lax.all_to_all(jnp.broadcast_to(shard[None], (size, *shard.shape)), axis,...]
    dot_general x21 -> x0, matrix products: 22.2 us -> none  [the longest x4 6.06 us: shards(): transform_panel = transform_panel - jnp.dot(scaled, joined, precision=high)]
    reduce_sum x9 -> x0, other arithmetic: 3.38 us -> none  [the longest x1 2.45 us: total_of_pieces(): return lax.all_gather(shard, axis).sum(0)]
    broadcast_in_dim x8 -> x0, local copies, waits for them, and re-layouts: 3.06 us -> none  [from_everyone(): jnp.broadcast_to(shard[None], (size, *shard.shape))]
  transfers between devices with their start and end apart: 8 -> 0, of which waited for: 7 -> 0; matrix products, arithmetic and copies ran while one was open for 4% -> 0% of each run, Pallas kernels for 0% -> 0%
where the time goes in v1:
time: 127 us; the launch traced here: 126 us
  Pallas kernels  122 us (96%)
  other arithmetic  2.41 us (2%)
  between operations  1.31 us (1%)
    pallas_call x1, Pallas kernels, shards(): pl.pallas_call(functools.partial(kernel, groups, ring), out_shape=jax.Sha...  122 us

profile of v1, /device:TPU:1, one launch (start us, length us, event | category | flops | bytes accessed | tf_op | source)
XLA Modules:
  0.0 126.3 jit_solution(4093766987256760598)
XLA Ops:
  1.3 122.0 %back_transform.1 = f32[1,32,16,512]{3,2,1,0:T(8,128)} custom-call(f32[1,32,16,512]{3,2,1,0:T(8,128)} %columns.1, bf16[1,8,128,512]{3,2,1,0:T(8,128)(2,1)} %vectors.1, f32[1,8,128,128]{3,2,1,0:T(8,128)} %factors.1, s32[1]{0:T(128)S(6)} %copy.7.order, s32[1]{0:T(128)S(6)} %copy.8.blocks), custom_call_target="tpu_custom_call" | custom-call | tf_op jit(solution)/shard_map/back_transform/pallas_call | solution.py:403
  123.3 0.0 copy-start
  123.3 0.6 copy-done
  123.9 0.1 iota_compare_fusion
  124.0 2.3 %broadcast_select_fusion = f32[1,32,16,512]{3,2,1,0:T(8,128)} fusion(f32[1,32,16,512]{3,2,1,0:T(8,128)} %back_transform.1, pred[32,16]{1,0:T(8,128)(4,1)S(1)} %iota_compare_fusion), kind=kLoop, calls=%fused_computation | loop fusion | flops 262144 | bytes 2097664 | tf_op jit(solution)/shard_map/jit(_where)/select_n | solution.py:442
Async XLA Ops:
  123.3 0.7 copy-start

commit v2 on v1

v2 whole, which is shorter than its diff:
```python
import functools

import jax
import jax.numpy as jnp
from jax import lax
from jax.experimental import pallas as pl
from jax.experimental.pallas import tpu as pltpu
from jax.sharding import PartitionSpec as P

MESH = pl.DeviceIdType.MESH
F32 = jnp.float32
BF16 = jnp.bfloat16
STREAMS = 2
GRAM_CUTS = 4
PART_CUTS = 2


def halves(x):
    first = x.astype(BF16)
    return first, (x - first.astype(F32)).astype(BF16)


def times(a, b):
    return jnp.dot(a, b, preferred_element_type=F32)


def product(a, b):
    return times(a[1], b[0]) + times(a[0], b[1]) + times(a[0], b[0])


def against(a, b):
    return lax.dot_general(a, b, (((1,), (1,)), ((), ())), preferred_element_type=F32)


def tree(ring):
    long = ring // 2
    up = {k: k - 1 for k in range(1, long + 1)}
    up.update({-k: 1 - k for k in range(1, ring - long)})
    if long == 4:
        up[3] = 1
    levels, left = [], set(up)
    while left:
        now = [k for k in left if not any(up[c] == k for c in left)]
        levels.append(sorted(now, key=lambda k: -abs(k)))
        left -= set(now)
    return levels, up


class Place:
    def __init__(self, ring):
        self.ring = ring
        self.levels, self.up = tree(ring)
        self.edges = sorted(self.up)
        strides = {k - self.up[k] for k in self.edges}
        self.near = sorted(strides | {-stride for stride in strides})
        self.group = lax.axis_index("group")
        self.section = lax.axis_index("section")
        self.z = self.section // 2
        self.core = lax.rem(self.section, 2)
        self.way = 1 - 2 * self.core

    def at(self, steps):
        return lax.rem(self.z + self.way * steps + 2 * self.ring, self.ring)

    def neighbour(self, steps):
        return (self.group, self.at(steps) * 2 + self.core)

    def partner(self):
        return (self.group, self.z * 2 + 1 - self.core)


class Sum:
    def __init__(self, place, cuts, src, swapped, landed, full, sent, swap_sem, ring_sem, gather_sem):
        self.p, self.cuts = place, cuts
        self.src, self.swapped, self.landed, self.full = src, swapped, landed, full
        self.sent, self.swap_sem, self.ring_sem, self.gather_sem = sent, swap_sem, ring_sem, gather_sem
        self.rows = landed.shape[1]
        self.part = self.rows // cuts

    def piece(self, ref, z, core, cut=None):
        start = pl.multiple_of((z * 2 + core) * self.rows, self.part)
        if cut is None:
            return ref.at[pl.ds(start, self.rows)]
        return ref.at[pl.ds(pl.multiple_of(start + cut * self.part, self.part), self.part)]

    def some(self, ref, at, cut):
        return ref.at[at, pl.ds(cut * self.part, self.part)]

    def send(self, src, dst, which, recv, device):
        return pltpu.make_async_remote_copy(
            src_ref=src,
            dst_ref=dst,
            send_sem=self.sent.at[which],
            recv_sem=recv,
            device_id=device,
            device_id_type=MESH,
        )

    def arrived(self, dst, recv):
        self.send(dst, dst, 0, recv, self.p.partner()).wait_recv()

    def swap(self):
        p = self.p
        for k in [k for level in p.levels for k in level] + [0]:
            z = p.at(-k)
            self.send(
                self.piece(self.src, z, 1 - p.core), self.swapped.at[z], 0, self.swap_sem.at[0, z], p.partner()
            ).start()

    def own(self, z, cut):
        return self.piece(self.src, z, self.p.core, cut)[...] + self.some(self.swapped, z, cut)[...]

    def gain(self, k, z, cut):
        value = self.own(z, cut)
        for e, below in enumerate(self.p.edges):
            if self.p.up[below] == k:
                part = self.some(self.landed, e, cut)
                self.arrived(part, self.ring_sem.at[e, cut])
                value = value + part[...]
        return value

    def step(self, level):
        p = self.p
        for k in p.levels[level]:
            z = p.at(k)
            self.arrived(self.swapped.at[z], self.swap_sem.at[0, z])
        for cut in range(self.cuts):
            for k in p.levels[level]:
                z, e = p.at(k), p.edges.index(k)
                source = self.some(self.swapped, z, cut)
                source[...] = self.gain(k, z, cut)
                self.send(
                    source, self.some(self.landed, e, cut), 0, self.ring_sem.at[e, cut], p.neighbour(k - p.up[k])
                ).start()

    def total(self, cut):
        p = self.p
        if cut == 0:
            self.arrived(self.swapped.at[p.z], self.swap_sem.at[0, p.z])
        return self.gain(0, p.z, cut)

    def forward(self, k, cut):
        p = self.p
        origin = p.at(-k)
        part = self.piece(self.full, origin, p.core, cut)
        if k:
            self.arrived(part, self.gather_sem.at[p.edges.index(k), cut])
        for e, beyond in sorted(enumerate(p.edges), key=lambda pair: -abs(pair[1])):
            if p.up[beyond] == k:
                self.send(part, part, 1, self.gather_sem.at[e, cut], p.neighbour(beyond - k)).start()
        self.send(part, part, 1, self.swap_sem.at[1, origin], p.partner()).start()

    def spread(self, value, cut):
        p = self.p
        self.piece(self.full, p.z, p.core, cut)[...] = value
        self.forward(0, cut)

    def relay(self, level):
        for cut in range(self.cuts):
            for k in self.p.levels[len(self.p.levels) - level]:
                self.forward(k, cut)

    def gathered(self):
        p = self.p
        for z in range(p.ring):
            self.arrived(self.piece(self.full, z, 1 - p.core), self.swap_sem.at[1, z])

    def drain(self):
        pieces = 2 * self.p.ring - 1
        whole = self.full.at[pl.ds(0, pieces * self.rows)]
        for which in range(2):
            self.send(whole, whole, which, self.swap_sem.at[0, 0], self.p.partner()).wait_send()


def kernel(
    groups,
    ring,
    columns,
    vectors,
    factors,
    order,
    blocks,
    out,
    raw,
    facts,
    basis,
    panel,
    moved,
    g_src,
    g_swapped,
    g_landed,
    g_full,
    turned,
    scaled,
    w_src,
    w_swapped,
    w_landed,
    w_full,
    load_sem,
    in_send,
    in_recv,
    out_send,
    out_recv,
    sent,
    swap_sem,
    gram_ring,
    gram_gather,
    ring_sem,
    gather_sem,
):
    p = Place(ring)
    me, section = p.group, p.section
    count, width, rows = raw.shape
    slots = panel.shape[1] // groups

    barrier = pltpu.get_barrier_semaphore()

    def greet(d, carry):
        peer = lax.rem(me + d, groups)
        pl.semaphore_signal(barrier, inc=1, device_id=(peer, section), device_id_type=MESH)
        return carry

    lax.fori_loop(1, groups, greet, 0)
    for other in [p.neighbour(stride) for stride in p.near] + [p.partner()]:
        pl.semaphore_signal(barrier, inc=1, device_id=other, device_id_type=MESH)

    loads = [
        pltpu.make_async_copy(vectors.at[0], raw, load_sem.at[0]),
        pltpu.make_async_copy(factors.at[0], facts, load_sem.at[1]),
    ]
    for s in range(STREAMS):
        loads.append(
            pltpu.make_async_copy(
                columns.at[0, me, pl.ds(s * slots, slots)],
                panel.at[s, pl.ds(pl.multiple_of(me * slots, slots), slots)],
                load_sem.at[2 + s],
            )
        )
    for load in loads:
        load.start()
    loads[0].wait()
    row = section * rows + lax.broadcasted_iota(jnp.int32, (width, rows), 1)
    inside = row < order[0]
    for j in range(count):
        block = jnp.where(inside, raw[j].astype(F32), 0.0)
        basis[pl.ds(j * width, width)] = block.astype(BF16)

    def exchange(s, source, target, send_sem, recv_sem):
        def one(k, carry):
            half = (k + 1) // 2
            d = groups // 2 + (2 * lax.rem(k, 2) - 1) * half
            peer = lax.rem(me + d, groups)
            pltpu.make_async_remote_copy(
                src_ref=source(peer),
                dst_ref=target(me),
                send_sem=send_sem,
                recv_sem=recv_sem,
                device_id=(peer, section),
                device_id_type=MESH,
            ).start()
            return carry

        lax.fori_loop(0, groups - 1, one, 0)

    def lines(ref, s):
        return lambda g: ref.at[s, pl.ds(pl.multiple_of(g * slots, slots), slots)]

    def slab(ref, s):
        return lambda g: ref.at[0, g, pl.ds(s * slots, slots)]

    place_of = {}
    for k in range(1, count):
        low = against(basis[pl.ds(k * width, width)], basis[pl.ds(0, k * width)])
        for j in range(k):
            place_of[k, j] = len(place_of)
            g_src[pl.ds(place_of[k, j] * width, width)] = low[:, j * width : (j + 1) * width]

    gram = Sum(
        p, GRAM_CUTS, g_src, g_swapped, g_landed, g_full, sent.at[0], swap_sem.at[0], gram_ring, gram_gather
    )
    parts = [
        Sum(
            p,
            PART_CUTS,
            w_src.at[s],
            w_swapped.at[s],
            w_landed.at[s],
            w_full.at[s],
            sent.at[1 + s],
            swap_sem.at[1 + s],
            ring_sem.at[s],
            gather_sem.at[s],
        )
        for s in range(STREAMS)
    ]
    pl.semaphore_wait(barrier, groups + len(p.near))
    gram.swap()
    exchange(0, slab(columns, 0), lines(panel, 0), in_send.at[0], in_recv.at[0])
    gram.step(0)
    for s in range(1, STREAMS):
        exchange(s, slab(columns, s), lines(panel, s), in_send.at[s], in_recv.at[s])
    loads[1].wait()
    for j in range(count):
        factor = jnp.where(j < blocks[0], facts[j], 0.0)
        turned[j] = factor.T
    gram.step(1)
    gram.step(2)
    def substitute(j):
        here, before = pl.ds(j * width, width), pl.ds(0, j * width)
        value = basis[here].astype(F32)
        if j:
            crossed = [g_full[pl.ds(place_of[j, i] * width, width)] for i in range(j)]
            crossed = halves(jnp.concatenate(crossed, axis=1))
            value = value - product(crossed, (scaled[0, before], scaled[1, before]))
        for i, part in enumerate(halves(product(halves(turned[j]), halves(value)))):
            scaled[i, here] = part

    def peer_lines(s):
        whole = panel.at[s, pl.ds(0, (groups - 1) * slots)]
        return whole

    def bring(s):
        loads[2 + s].wait()
        whole = peer_lines(s)
        pltpu.make_async_remote_copy(
            whole, whole, in_send.at[s], in_recv.at[s], device_id=p.partner(), device_id_type=MESH
        ).wait_recv()
        a, b = halves(panel[s])
        v = basis[...]
        w_src[s] = against(b, v) + against(a, v)

    def leave(s):
        moved[s] = panel[s] - product(halves(w_full[s]), (scaled[0], scaled[1]))
        exchange(s, lines(moved, s), slab(out, s), out_send.at[s], out_recv.at[s])
        own = pltpu.make_async_copy(lines(moved, s)(me), slab(out, s)(me), load_sem.at[2 + s])
        own.start()
        return own

    def finish(s):
        for cut in range(PART_CUTS):
            parts[s].spread(parts[s].total(cut), cut)

    bring(0)
    parts[0].swap()
    for cut in range(GRAM_CUTS):
        gram.spread(gram.total(cut), cut)
    parts[0].step(0)
    gram.relay(1)
    parts[0].step(1)
    gram.relay(2)
    parts[0].step(2)
    bring(1)
    parts[1].swap()
    gram.relay(3)
    finish(0)
    parts[1].step(0)
    gram.gathered()
    for j in range(0, 3):
        substitute(j)
    parts[0].relay(1)
    parts[1].step(1)
    for j in range(3, 6):
        substitute(j)
    parts[0].relay(2)
    parts[1].step(2)
    for j in range(6, count):
        substitute(j)
    parts[0].relay(3)
    finish(1)
    parts[0].gathered()
    own0 = leave(0)
    parts[1].relay(1)
    parts[1].relay(2)
    parts[1].relay(3)
    parts[1].gathered()
    own1 = leave(1)

    gram.drain()
    for s in range(STREAMS):
        parts[s].drain()
    own0.wait()
    own1.wait()
    for s in range(STREAMS):
        whole = peer_lines(s)
        pltpu.make_async_remote_copy(
            whole, whole, in_send.at[s], in_recv.at[s], device_id=p.partner(), device_id_type=MESH
        ).wait_send()
        there = pltpu.make_async_remote_copy(
            whole, whole, out_send.at[s], out_recv.at[s], device_id=p.partner(), device_id_type=MESH
        )
        there.wait_send()
        there.wait_recv()


def shards(groups, ring, columns, vectors, factors, order, blocks, live):
    _, count, width, rows = vectors.shape
    slots = columns.shape[2]
    each = slots // STREAMS
    lines = groups * each
    merged = count * width
    gram = count * (count - 1) // 2 * width
    g_piece, w_piece = gram // (2 * ring), lines // (2 * ring)
    anywhere = pl.BlockSpec(memory_space=pl.ANY)
    scalars = pl.BlockSpec(memory_space=pltpu.SMEM)
    returned = pl.pallas_call(
        functools.partial(kernel, groups, ring),
        out_shape=jax.ShapeDtypeStruct(columns.shape, F32),
        in_specs=[anywhere, anywhere, anywhere, scalars, scalars],
        out_specs=anywhere,
        scratch_shapes=[
            pltpu.VMEM((count, width, rows), BF16),
            pltpu.VMEM((count, width, width), F32),
            pltpu.VMEM((merged, rows), BF16),
            pltpu.VMEM((STREAMS, lines, rows), F32),
            pltpu.VMEM((STREAMS, lines, rows), F32),
            pltpu.VMEM((gram, width), F32),
            pltpu.VMEM((ring, g_piece, width), F32),
            pltpu.VMEM((ring - 1, g_piece, width), F32),
            pltpu.VMEM((gram, width), F32),
            pltpu.VMEM((count, width, width), F32),
            pltpu.VMEM((2, merged, rows), BF16),
            pltpu.VMEM((STREAMS, lines, merged), F32),
            pltpu.VMEM((STREAMS, ring, w_piece, merged), F32),
            pltpu.VMEM((STREAMS, ring - 1, w_piece, merged), F32),
            pltpu.VMEM((STREAMS, lines, merged), F32),
            pltpu.SemaphoreType.DMA((2 + STREAMS,)),
            pltpu.SemaphoreType.DMA((STREAMS,)),
            pltpu.SemaphoreType.DMA((STREAMS,)),
            pltpu.SemaphoreType.DMA((STREAMS,)),
            pltpu.SemaphoreType.DMA((STREAMS,)),
            pltpu.SemaphoreType.DMA((1 + STREAMS, 2)),
            pltpu.SemaphoreType.DMA((1 + STREAMS, 2, ring)),
            pltpu.SemaphoreType.DMA((ring - 1, GRAM_CUTS)),
            pltpu.SemaphoreType.DMA((ring - 1, GRAM_CUTS)),
            pltpu.SemaphoreType.DMA((STREAMS, ring - 1, PART_CUTS)),
            pltpu.SemaphoreType.DMA((STREAMS, ring - 1, PART_CUTS)),
        ],
        compiler_params=pltpu.CompilerParams(
            collective_id=0, has_side_effects=True, vmem_limit_bytes=60 * 1024 * 1024
        ),
        name="back_transform",
    )(columns, vectors, factors, order, blocks)
    keep = jnp.arange(slots)[None, :] < live[0][:, None]
    return jnp.where(keep[None, :, :, None], returned, jnp.float32(0.0))


def solution(mesh):
    groups, ring = mesh.shape["group"], mesh.shape["section"] // 2
    placed = (
        P("group", None, None, "section"),
        P("group", None, None, "section"),
        P("group", None, None, None),
        P("group"),
        P("group"),
        P("group", None),
    )
    return jax.shard_map(
        functools.partial(shards, groups, ring),
        mesh=mesh,
        in_specs=placed,
        out_specs=P("group", None, None, "section"),
        check_vma=False,
    )
```

time: 127 us -> 99.9 us (0.79)
  Pallas kernels: 122 us -> 95.3 us
    pallas_call x1, Pallas kernels: 122 us -> 95.3 us  [shards(): pl.pallas_call(functools.partial(kernel, groups, ring), out_shape=jax.Sha...]
where the time goes in v2:
time: 99.9 us; the launch traced here: 99.7 us
  Pallas kernels  95.3 us (95%)
  other arithmetic  2.41 us (2%)
  between operations  1.31 us (1%)
    pallas_call x1, Pallas kernels, shards(): pl.pallas_call(functools.partial(kernel, groups, ring), out_shape=jax.Sha...  95.3 us
    select_n x1, other arithmetic, shards(): return jnp.where(keep[None, :, :, None], returned, jnp.float32(0.0))  2.34 us

profile of v2, /device:TPU:1, one launch (start us, length us, event | category | flops | bytes accessed | tf_op | source)
XLA Modules:
  0.0 99.7 jit_solution(6971930627143398331)
XLA Ops:
  1.3 95.3 %back_transform.1 = f32[1,32,16,512]{3,2,1,0:T(8,128)} custom-call(f32[1,32,16,512]{3,2,1,0:T(8,128)} %columns.1, bf16[1,8,128,512]{3,2,1,0:T(8,128)(2,1)} %vectors.1, f32[1,8,128,128]{3,2,1,0:T(8,128)} %factors.1, s32[1]{0:T(128)S(6)} %copy.7.order, s32[1]{0:T(128)S(6)} %copy.8.blocks), custom_call_target="tpu_custom_call" | custom-call | tf_op jit(solution)/shard_map/back_transform/pallas_call | solution.py:405
  96.6 0.0 copy-start
  96.6 0.6 copy-done
  97.3 0.1 iota_compare_fusion
  97.4 2.3 %broadcast_select_fusion = f32[1,32,16,512]{3,2,1,0:T(8,128)} fusion(f32[1,32,16,512]{3,2,1,0:T(8,128)} %back_transform.1, pred[32,16]{1,0:T(8,128)(4,1)S(1)} %iota_compare_fusion), kind=kLoop, calls=%fused_computation | loop fusion | flops 262144 | bytes 2097664 | tf_op jit(solution)/shard_map/jit(_where)/select_n | solution.py:444
Async XLA Ops:
  96.6 0.7 copy-start

commit v3 on v2

--- a/solution.py
+++ b/solution.py
@@ -32,11 +32,11 @@
     return lax.dot_general(a, b, (((1,), (1,)), ((), ())), preferred_element_type=F32)
 
 
-def tree(ring):
+def tree(ring, skip):
     long = ring // 2
     up = {k: k - 1 for k in range(1, long + 1)}
     up.update({-k: 1 - k for k in range(1, ring - long)})
-    if long == 4:
+    if skip and long == 4:
         up[3] = 1
     levels, left = [], set(up)
     while left:
@@ -49,9 +49,8 @@
 class Place:
     def __init__(self, ring):
         self.ring = ring
-        self.levels, self.up = tree(ring)
-        self.edges = sorted(self.up)
-        strides = {k - self.up[k] for k in self.edges}
+        up = tree(ring, True)[1]
+        strides = {k - up[k] for k in up} | {1}
         self.near = sorted(strides | {-stride for stride in strides})
         self.group = lax.axis_index("group")
         self.section = lax.axis_index("section")
@@ -70,8 +69,10 @@
 
 
 class Sum:
-    def __init__(self, place, cuts, src, swapped, landed, full, sent, swap_sem, ring_sem, gather_sem):
+    def __init__(self, place, skip, cuts, src, swapped, landed, full, sent, swap_sem, ring_sem, gather_sem):
         self.p, self.cuts = place, cuts
+        self.levels, self.up = tree(place.ring, skip)
+        self.edges = sorted(self.up)
         self.src, self.swapped, self.landed, self.full = src, swapped, landed, full
         self.sent, self.swap_sem, self.ring_sem, self.gather_sem = sent, swap_sem, ring_sem, gather_sem
         self.rows = landed.shape[1]
@@ -101,7 +102,7 @@
 
     def swap(self):
         p = self.p
-        for k in [k for level in p.levels for k in level] + [0]:
+        for k in [k for level in self.levels for k in level] + [0]:
             z = p.at(-k)
             self.send(
                 self.piece(self.src, z, 1 - p.core), self.swapped.at[z], 0, self.swap_sem.at[0, z], p.partner()
@@ -112,8 +113,8 @@
 
     def gain(self, k, z, cut):
         value = self.own(z, cut)
-        for e, below in enumerate(self.p.edges):
-            if self.p.up[below] == k:
+        for e, below in enumerate(self.edges):
+            if self.up[below] == k:
                 part = self.some(self.landed, e, cut)
                 self.arrived(part, self.ring_sem.at[e, cut])
                 value = value + part[...]
@@ -121,16 +122,16 @@
 
     def step(self, level):
         p = self.p
-        for k in p.levels[level]:
+        for k in self.levels[level]:
             z = p.at(k)
             self.arrived(self.swapped.at[z], self.swap_sem.at[0, z])
         for cut in range(self.cuts):
-            for k in p.levels[level]:
-                z, e = p.at(k), p.edges.index(k)
+            for k in self.levels[level]:
+                z, e = p.at(k), self.edges.index(k)
                 source = self.some(self.swapped, z, cut)
                 source[...] = self.gain(k, z, cut)
                 self.send(
-                    source, self.some(self.landed, e, cut), 0, self.ring_sem.at[e, cut], p.neighbour(k - p.up[k])
+                    source, self.some(self.landed, e, cut), 0, self.ring_sem.at[e, cut], p.neighbour(k - self.up[k])
                 ).start()
 
     def total(self, cut):
@@ -144,9 +145,9 @@
         origin = p.at(-k)
         part = self.piece(self.full, origin, p.core, cut)
         if k:
-            self.arrived(part, self.gather_sem.at[p.edges.index(k), cut])
-        for e, beyond in sorted(enumerate(p.edges), key=lambda pair: -abs(pair[1])):
-            if p.up[beyond] == k:
+            self.arrived(part, self.gather_sem.at[self.edges.index(k), cut])
+        for e, beyond in sorted(enumerate(self.edges), key=lambda pair: -abs(pair[1])):
+            if self.up[beyond] == k:
                 self.send(part, part, 1, self.gather_sem.at[e, cut], p.neighbour(beyond - k)).start()
         self.send(part, part, 1, self.swap_sem.at[1, origin], p.partner()).start()
 
@@ -157,7 +158,7 @@
 
     def relay(self, level):
         for cut in range(self.cuts):
-            for k in self.p.levels[len(self.p.levels) - level]:
+            for k in self.levels[len(self.levels) - level]:
                 self.forward(k, cut)
 
     def gathered(self):
@@ -276,11 +277,12 @@
             g_src[pl.ds(place_of[k, j] * width, width)] = low[:, j * width : (j + 1) * width]
 
     gram = Sum(
-        p, GRAM_CUTS, g_src, g_swapped, g_landed, g_full, sent.at[0], swap_sem.at[0], gram_ring, gram_gather
+        p, False, GRAM_CUTS, g_src, g_swapped, g_landed, g_full, sent.at[0], swap_sem.at[0], gram_ring, gram_gather
     )
     parts = [
         Sum(
             p,
+            True,
             PART_CUTS,
             w_src.at[s],
             w_swapped.at[s],
@@ -297,14 +299,13 @@
     gram.swap()
     exchange(0, slab(columns, 0), lines(panel, 0), in_send.at[0], in_recv.at[0])
     gram.step(0)
-    for s in range(1, STREAMS):
-        exchange(s, slab(columns, s), lines(panel, s), in_send.at[s], in_recv.at[s])
     loads[1].wait()
     for j in range(count):
         factor = jnp.where(j < blocks[0], facts[j], 0.0)
         turned[j] = factor.T
     gram.step(1)
     gram.step(2)
+    gram.step(3)
     def substitute(j):
         here, before = pl.ds(j * width, width), pl.ds(0, j * width)
         value = basis[here].astype(F32)
@@ -340,6 +341,8 @@
         for cut in range(PART_CUTS):
             parts[s].spread(parts[s].total(cut), cut)
 
+    for s in range(1, STREAMS):
+        exchange(s, slab(columns, s), lines(panel, s), in_send.at[s], in_recv.at[s])
     bring(0)
     parts[0].swap()
     for cut in range(GRAM_CUTS):
@@ -354,6 +357,7 @@
     gram.relay(3)
     finish(0)
     parts[1].step(0)
+    gram.relay(4)
     gram.gathered()
     for j in range(0, 3):
         substitute(j)

time: 99.9 us -> 95.7 us (0.958)
  Pallas kernels: 95.3 us -> 91.1 us
    pallas_call x1, Pallas kernels: 95.3 us -> 91.1 us  [shards(): pl.pallas_call(functools.partial(kernel, groups, ring), out_shape=jax.Sha...]
where the time goes in v3:
time: 95.7 us; the launch traced here: 95.5 us
  Pallas kernels  91.1 us (95%)
  other arithmetic  2.41 us (3%)
  between operations  1.31 us (1%)
    pallas_call x1, Pallas kernels, shards(): pl.pallas_call(functools.partial(kernel, groups, ring), out_shape=jax.Sha...  91.1 us
    select_n x1, other arithmetic, shards(): return jnp.where(keep[None, :, :, None], returned, jnp.float32(0.0))  2.34 us

profile of v3, /device:TPU:1, one launch (start us, length us, event | category | flops | bytes accessed | tf_op | source)
XLA Modules:
  0.0 95.5 jit_solution(10613830336244450005)
XLA Ops:
  1.3 91.1 %back_transform.1 = f32[1,32,16,512]{3,2,1,0:T(8,128)} custom-call(f32[1,32,16,512]{3,2,1,0:T(8,128)} %columns.1, bf16[1,8,128,512]{3,2,1,0:T(8,128)(2,1)} %vectors.1, f32[1,8,128,128]{3,2,1,0:T(8,128)} %factors.1, s32[1]{0:T(128)S(6)} %copy.7.order, s32[1]{0:T(128)S(6)} %copy.8.blocks), custom_call_target="tpu_custom_call" | custom-call | tf_op jit(solution)/shard_map/back_transform/pallas_call | solution.py:409
  92.4 0.0 copy-start
  92.4 0.6 copy-done
  93.1 0.1 iota_compare_fusion
  93.1 2.3 %broadcast_select_fusion = f32[1,32,16,512]{3,2,1,0:T(8,128)} fusion(f32[1,32,16,512]{3,2,1,0:T(8,128)} %back_transform.1, pred[32,16]{1,0:T(8,128)(4,1)S(1)} %iota_compare_fusion), kind=kLoop, calls=%fused_computation | loop fusion | flops 262144 | bytes 2097664 | tf_op jit(solution)/shard_map/jit(_where)/select_n | solution.py:448
Async XLA Ops:
  92.4 0.7 copy-start
